TPU v7x, 32 devices: a whole 2x2x4 slice. The times are simulated.
32 devices in a mesh: shard: 4 (over x, core), replica: 8 (over z, y).
Axes of the slice: x: 2, y: 2, z: 4, core: 2. Of those that a mesh axis runs over, the one named last changes fastest.
Arguments:
- gradients: bfloat16 [8, 32, 512, 512], P('replica', 'shard'), may hold values from -3 to 3
- first_moment: float32 [32, 512, 512], P(('shard', 'replica')), may hold values from -6 to 6
- second_moment: float32 [32, 512, 512], P(('shard', 'replica')), may hold values from 0.25 to 4
- left_stat: float32 [32, 512, 512], P(('shard', 'replica')), as said below
- right_stat: float32 [32, 512, 512], P(('shard', 'replica')), as said below
- left_basis: float32 [32, 512, 512], P(('shard', 'replica')), as said below
- right_basis: float32 [32, 512, 512], P(('shard', 'replica')), as said below
- refresh_flags: int32 [32], replicated, may hold values from 0 to 1, as said below
Outputs:
- direction: bfloat16 [32, 512, 512], P('shard')
- new_first: float32 [32, 512, 512], P(('shard', 'replica'))
- new_second: float32 [32, 512, 512], P(('shard', 'replica'))
- new_left: float32 [32, 512, 512], P(('shard', 'replica'))
- new_right: float32 [32, 512, 512], P(('shard', 'replica'))
- new_left_basis: float32 [32, 512, 512], P(('shard', 'replica'))
- new_right_basis: float32 [32, 512, 512], P(('shard', 'replica'))
Inputs may be any that keep to these rules, and one draw needn't show every extreme that they name: Write b = ((p * 8 + q)) + j. For every q, j and k, exactly one of the two blocks with p = 2 k and p = 2 k + 1 has refresh_flags[b] = 1. `left_stat`: every block is symmetric positive definite with all eigenvalues 1 or more. `right_stat`: every block is symmetric positive definite with all eigenvalues 1 or more. `left_basis`: every block is an orthogonal matrix. `right_basis`: every block is an orthogonal matrix.
All inputs are finite; a program needn't handle non-finite values.
Results may differ from a plain program's by a relative error of at most 0.012.
Values may be sent and summed in bfloat16 or wider, within the bound.
A program may use at most 128 MiB of HBM per device.

v0:
```python
import jax
import jax.numpy as jnp
from jax import lax
from jax.sharding import PartitionSpec as P

POWER = 2


beta_one = 0.95
beta_two = 0.95
epsilon = 1e-08
bias_step = 10.0


def swapped(block, axis, stride):
    count = lax.axis_size(axis)
    route = []
    for low in range(count):
        high = low | 1 << stride
        if high != low and high < count:
            route += [(low, high), (high, low)]
    return lax.ppermute(block, axis, route)


def highest(left_side, right_side):
    return jnp.dot(
        left_side, right_side, precision=lax.Precision.HIGHEST, preferred_element_type=jnp.float32
    )


def orthonormal(matrix):
    gram = highest(matrix.T, matrix)
    lower_factor = jnp.linalg.cholesky(gram)
    return jax.scipy.linalg.solve_triangular(lower_factor, matrix.T, lower=True).T


def power_step(factor, basis):
    for repeat in range(POWER):
        product = jnp.dot(
            factor.astype(jnp.bfloat16),
            basis.astype(jnp.bfloat16),
            preferred_element_type=jnp.float32,
        )
        basis = orthonormal(product)
    return basis


def local(
    gradients,
    first_moment,
    second_moment,
    left_stat,
    right_stat,
    left_basis,
    right_basis,
    refresh_flags,
):
    replica_count = lax.axis_size("replica")
    shard_pos = lax.axis_index("shard")
    replica_pos = lax.axis_index("replica")
    summed = lax.psum_scatter(gradients, "replica", scatter_dimension=1, tiled=True).astype(
        jnp.float32
    )[0]
    per_device = summed.shape[0]
    block_side = summed.shape[1]
    low_grad = summed.astype(jnp.bfloat16)
    left_new = beta_two * left_stat + (1.0 - beta_two) / block_side * jnp.einsum(
        "kij,klj->kil", low_grad, low_grad, preferred_element_type=jnp.float32
    )
    right_new = beta_two * right_stat + (1.0 - beta_two) / block_side * jnp.einsum(
        "kji,kjl->kil", low_grad, low_grad, preferred_element_type=jnp.float32
    )
    owner_id = shard_pos * replica_count + replica_pos
    own_flags = lax.dynamic_slice_in_dim(refresh_flags, owner_id * per_device, per_device)
    renewed = (own_flags == 1)[:, None, None]
    partner_id = (shard_pos ^ 1) * replica_count + replica_pos
    partner_flags = lax.dynamic_slice_in_dim(refresh_flags, partner_id * per_device, per_device)
    pair_out = jnp.stack([right_new, right_basis], 1).astype(jnp.bfloat16)
    outgoing = jnp.where(renewed[:, :, :, None], pair_out, jnp.zeros_like(pair_out))
    incoming = swapped(outgoing, "shard", 0)
    position = 0
    lefts = [
        lax.cond(
            own_flags[position] == 1,
            lambda: power_step(left_new[position], left_basis[position]),
            lambda: left_basis[position],
        )
    ]
    helped = [
        lax.cond(
            partner_flags[position] == 1,
            lambda: power_step(incoming[position, 0], incoming[position, 1]),
            lambda: jnp.zeros(incoming.shape[2:], jnp.float32),
        )
    ]
    basis_left = jnp.stack(lefts, 0)
    arrived = swapped(jnp.stack(helped, 0).astype(jnp.bfloat16), "shard", 0).astype(jnp.float32)
    basis_right = jnp.where(renewed, arrived, right_basis)
    position = 0
    carried_list = [
        lax.cond(
            own_flags[position] == 1,
            lambda: highest(
                highest(
                    highest(basis_left[position].T, left_basis[position]), first_moment[position]
                ),
                highest(right_basis[position].T, basis_right[position]),
            ),
            lambda: first_moment[position],
        )
    ]
    carried = jnp.stack(carried_list, 0)
    rotated = jnp.einsum("kji,kjl->kil", basis_left, summed, precision=lax.Precision.HIGHEST)
    rotated = jnp.einsum("kil,klm->kim", rotated, basis_right, precision=lax.Precision.HIGHEST)
    moment_new = beta_one * carried + (1.0 - beta_one) * rotated
    second_new = beta_two * second_moment + (1.0 - beta_two) * rotated * rotated
    scaled = (
        moment_new
        / (1.0 - beta_one**bias_step)
        / (jnp.sqrt(second_new / (1.0 - beta_two**bias_step)) + epsilon)
    )
    outward = jnp.einsum("kij,kjl->kil", basis_left, scaled, precision=lax.Precision.HIGHEST)
    outward = jnp.einsum("kil,kml->kim", outward, basis_right, precision=lax.Precision.HIGHEST)
    gathered = lax.all_gather(outward.astype(jnp.bfloat16), "replica", axis=0, tiled=True)
    return (gathered, moment_new, second_new, left_new, right_new, basis_left, basis_right)


def solution(mesh):
    in_specs = (
        P("replica", "shard", None, None),
        P(("shard", "replica"), None, None),
        P(("shard", "replica"), None, None),
        P(("shard", "replica"), None, None),
        P(("shard", "replica"), None, None),
        P(("shard", "replica"), None, None),
        P(("shard", "replica"), None, None),
        P(),
    )
    out_specs = (
        P("shard", None, None),
        P(("shard", "replica"), None, None),
        P(("shard", "replica"), None, None),
        P(("shard", "replica"), None, None),
        P(("shard", "replica"), None, None),
        P(("shard", "replica"), None, None),
        P(("shard", "replica"), None, None),
    )
    return jax.shard_map(local, mesh=mesh, in_specs=in_specs, out_specs=out_specs, check_vma=False)
```

profile of v0, /device:TPU:0, one launch (start us, length us, event | category | flops | bytes accessed | tf_op | source)
XLA Modules:
  0.0 849.7 jit_solution(10542289103548135286)
XLA Ops:
  7.2 2.4 copy.96
  11.1 91.6 %reduce-scatter.2.cloned.1.call-done = bf16[1,1,512,512]{3,2,1,0:T(8,128)(2,1)} async-done(((bf16[1,8,512,512]{3,2,1,0:T(8,128)(2,1)}), bf16[1,1,512,512]{3,2,1,0:T(8,128)(2,1)}) %reduce-scatter.2.cloned.1.call-update) | async-done | bytes 524304 | tf_op jit(solution)/shard_map/reduce_scatter | solution.py:61
  107.5 318.5 %conditional.4 = (bf16[512,512]{0,1:T(8,128)(2,1)S(1)}) conditional(s32[]{:T(128)} %bitcast.62, () %tuple.33, bf16[1,2,512,512]{3,2,1,0:T(8,128)(2,1)} %collective-permute-done), branch_computations={%region_11.14_spmd, %region_12.15_spmd} | conditional | flops 6586237440 | bytes 55583216 | solution.py:90
  114.8 11.7 %cholesky.606 = f32[128,128]{1,0:T(8,128)S(1)} custom-call(f32[128,128]{1,0:T(8,128)S(1)} %cholesky.772), custom_call_target="Cholesky" | custom-call | tf_op jit(solution)/shard_map/cond/branch_1_fun/jit(cholesky)/cholesky | solution.py:33
  126.6 9.8 %custom-call.43 = f32[1,128,128]{1,2,0:T(8,128)S(1)} custom-call(f32[1,128,128]{2,1,0:T(8,128)S(1)} %get-tuple-element.175), custom_call_target="InvertDiagBlocksLowerTriangular" | custom-call | tf_op jit(solution)/shard_map/cond/branch_1_fun/jit(cholesky)/cholesky | solution.py:33
  139.0 12.0 %cholesky.625 = f32[128,128]{1,0:T(8,128)S(1)} custom-call(f32[128,128]{1,0:T(8,128)S(1)} %cholesky.776), custom_call_target="Cholesky" | custom-call | tf_op jit(solution)/shard_map/cond/branch_1_fun/jit(cholesky)/cholesky | solution.py:33
  153.0 9.8 %custom-call.44 = f32[1,128,128]{1,2,0:T(8,128)S(1)} custom-call(f32[1,128,128]{2,1,0:T(8,128)S(1)} %get-tuple-element.172), custom_call_target="InvertDiagBlocksLowerTriangular" | custom-call | tf_op jit(solution)/shard_map/cond/branch_1_fun/jit(cholesky)/cholesky | solution.py:33
  164.4 11.7 %cholesky.646 = f32[128,128]{1,0:T(8,128)S(1)} custom-call(f32[128,128]{1,0:T(8,128)S(1)} %cholesky.781), custom_call_target="Cholesky" | custom-call | tf_op jit(solution)/shard_map/cond/branch_1_fun/jit(cholesky)/cholesky | solution.py:33
  177.4 9.8 %custom-call.45 = f32[1,128,128]{1,2,0:T(8,128)S(1)} custom-call(f32[1,128,128]{2,1,0:T(8,128)S(1)} %get-tuple-element.169), custom_call_target="InvertDiagBlocksLowerTriangular" | custom-call | tf_op jit(solution)/shard_map/cond/branch_1_fun/jit(cholesky)/cholesky | solution.py:33
  188.7 23.3 %cholesky.663 = f32[128,128]{1,0:T(8,128)S(1)} custom-call(f32[128,128]{1,0:T(8,128)S(1)} %convolution_subtract_fusion.23), custom_call_target="Cholesky" | custom-call | tf_op jit(solution)/shard_map/cond/branch_1_fun/jit(cholesky)/cholesky | solution.py:33
  214.4 11.6 %while.10 = (s32[]{:T(128)}, f32[512,512]{1,0:T(8,128)}, s32[4,2]{0,1:T(2,128)S(1)}, f32[4,128,128]{2,1,0:T(8,128)S(1)}, s32[]{:T(128)}) while((s32[]{:T(128)}, f32[512,512]{1,0:T(8,128)}, s32[4,2]{0,1:T(2,128)S(1)}, f32[4,128,128]{2,1,0:T(8,128)S(1)}, s32[]{:T(128)}) %tuple.129), condition=%wide.while_cond.clone.1, body=%wide.while_body.clone.1.sunk | while | flops 2 | bytes 131189 | solution.py:34
  226.0 39.3 %custom-call.46 = f32[4,128,128]{1,2,0:T(8,128)S(1)} custom-call(f32[4,128,128]{2,1,0:T(8,128)S(1)} %get-tuple-element.73), custom_call_target="InvertDiagBlocksLowerTriangular" | custom-call | tf_op jit(solution)/shard_map/cond/branch_1_fun/jit(_solve_triangular)/triangular_solve | solution.py:34
  270.0 2.4 convolution_subtract_fusion.17
  279.9 11.7 %cholesky.678 = f32[128,128]{1,0:T(8,128)S(1)} custom-call(f32[128,128]{1,0:T(8,128)S(1)} %cholesky.785), custom_call_target="Cholesky" | custom-call | tf_op jit(solution)/shard_map/cond/branch_1_fun/jit(cholesky)/cholesky | solution.py:33
  292.3 10.2 %custom-call.47 = f32[1,128,128]{1,2,0:T(8,128)S(1)} custom-call(f32[1,128,128]{2,1,0:T(8,128)S(1)} %get-tuple-element.165), custom_call_target="InvertDiagBlocksLowerTriangular" | custom-call | tf_op jit(solution)/shard_map/cond/branch_1_fun/jit(cholesky)/cholesky | solution.py:33
  305.1 11.7 %cholesky.697 = f32[128,128]{1,0:T(8,128)S(1)} custom-call(f32[128,128]{1,0:T(8,128)S(1)} %cholesky.789), custom_call_target="Cholesky" | custom-call | tf_op jit(solution)/shard_map/cond/branch_1_fun/jit(cholesky)/cholesky | solution.py:33
  318.8 9.8 %custom-call.48 = f32[1,128,128]{1,2,0:T(8,128)S(1)} custom-call(f32[1,128,128]{2,1,0:T(8,128)S(1)} %get-tuple-element.162), custom_call_target="InvertDiagBlocksLowerTriangular" | custom-call | tf_op jit(solution)/shard_map/cond/branch_1_fun/jit(cholesky)/cholesky | solution.py:33
  330.2 11.7 %cholesky.718 = f32[128,128]{1,0:T(8,128)S(1)} custom-call(f32[128,128]{1,0:T(8,128)S(1)} %cholesky.794), custom_call_target="Cholesky" | custom-call | tf_op jit(solution)/shard_map/cond/branch_1_fun/jit(cholesky)/cholesky | solution.py:33
  343.2 9.9 %custom-call.49 = f32[1,128,128]{1,2,0:T(8,128)S(1)} custom-call(f32[1,128,128]{2,1,0:T(8,128)S(1)} %get-tuple-element.159), custom_call_target="InvertDiagBlocksLowerTriangular" | custom-call | tf_op jit(solution)/shard_map/cond/branch_1_fun/jit(cholesky)/cholesky | solution.py:33
  354.6 11.7 %cholesky.735 = f32[128,128]{1,0:T(8,128)S(1)} custom-call(f32[128,128]{1,0:T(8,128)S(1)} %convolution_subtract_fusion.22), custom_call_target="Cholesky" | custom-call | tf_op jit(solution)/shard_map/cond/branch_1_fun/jit(cholesky)/cholesky | solution.py:33
  368.7 11.6 %while.11 = (s32[]{:T(128)}, f32[512,512]{1,0:T(8,128)}, s32[4,2]{0,1:T(2,128)S(1)}, f32[4,128,128]{2,1,0:T(8,128)S(1)}, s32[]{:T(128)}) while((s32[]{:T(128)}, f32[512,512]{1,0:T(8,128)}, s32[4,2]{0,1:T(2,128)S(1)}, f32[4,128,128]{2,1,0:T(8,128)S(1)}, s32[]{:T(128)}) %tuple.157), condition=%wide.while_cond.clone.2, body=%wide.while_body.clone.2.sunk | while | flops 2 | bytes 131189 | solution.py:34
  380.3 39.3 %custom-call.50 = f32[4,128,128]{1,2,0:T(8,128)S(1)} custom-call(f32[4,128,128]{2,1,0:T(8,128)S(1)} %get-tuple-element.74), custom_call_target="InvertDiagBlocksLowerTriangular" | custom-call | tf_op jit(solution)/shard_map/cond/branch_1_fun/jit(_solve_triangular)/triangular_solve | solution.py:34
  427.0 3.0 fusion.165
  430.0 10.6 %conditional.3 = (f32[512,512]{0,1:T(8,128)S(1)}, f32[1,512,512]{1,2,0:T(8,128)}) conditional(s32[]{:T(128)} %convert_element_type.74, (f32[1,512,512]{2,1,0:T(8,128)S(1)}) %tuple.154, (f32[1,512,512]{2,1,0:T(8,128)}, f32[1,512,512]{2,1,0:T(8,128)S(1)}) %tuple.155), branch_computations={%region_1.2_spmd, %region_2.13_spmd} | conditional | flops 6585713152 | bytes 58991096 | solution.py:83
  440.5 3.0 fusion.178
  446.1 3.5 fusion.168
  449.6 4.0 fusion.169
  453.7 2.7 convolution_convert_fusion
  456.4 2.5 copy.22
  458.9 2.4 fusion.185
  461.3 376.6 %all-gather.3.cloned.1.call-done = bf16[4096,512]{1,0:T(8,128)(2,1)} async-done(((bf16[512,512]{1,0:T(8,128)(2,1)}), bf16[4096,512]{1,0:T(8,128)(2,1)}) %all-gather.3.cloned.1.call-update) | async-done | bytes 4194320 | tf_op jit(solution)/shard_map/all_gather | solution.py:124
  837.9 4.5 copy.97
  (123 shorter events, 76.2 us)
Async XLA Ops:
  7.2 95.5 %copy-start.9 = (f32[1,512,512]{2,1,0:T(8,128)S(1)}, f32[1,512,512]{2,1,0:T(8,128)}, u32[]{:S(2)}) copy-start(f32[1,512,512]{2,1,0:T(8,128)} %param.21) | copy-start | bytes 3145732
  7.2 3.8 copy-start.2
  7.2 2.5 copy-start.10
  7.2 95.5 %reduce-scatter.2.cloned.1.call-start = ((), (), s32[]{:S(2)}) async-start(), calls=%async_computation.1 | async-start | bytes 4718592 | tf_op jit(solution)/shard_map/reduce_scatter | solution.py:61
  9.7 828.3 %all-gather.3.cloned.1.call-start = ((), (), s32[]{:S(2)}) async-start(), calls=%async_computation.2 | async-start | bytes 4718592 | tf_op jit(solution)/shard_map/all_gather | solution.py:124
  104.4 3.1 copy-start.3
  104.6 2.9 collective-permute-start
  107.5 322.5 %copy-start.1 = (f32[1,512,512]{2,1,0:T(8,128)S(1)}, f32[1,512,512]{2,1,0:T(8,128)}, u32[]{:S(2)}) copy-start(f32[1,512,512]{2,1,0:T(8,128)} %param.22) | copy-start | bytes 3145732
  113.8 1.0 copy-start.4
  278.9 1.0 copy-start.6
  427.0 16.6 %collective-permute-start.1 = (bf16[1,512,512]{2,1,0:T(8,128)(2,1)}, bf16[1,512,512]{2,1,0:T(8,128)(2,1)}, u32[]{:S(2)}, u32[]{:S(2)}) collective-permute-start(bf16[1,512,512]{2,1,0:T(8,128)(2,1)} %bitcast.222), channel_id=1, source_target_pairs={{0,8},{8,0},{16,24},{24,16},{1,9},{9,1},{17,25},{25,17},{2,10},{10... | collective-permute-start | bytes 1572872 | tf_op jit(solution)/shard_map/ppermute | solution.py:22
  445.0 8.6 %copy-start = (f32[1,512,512]{2,1,0:T(8,128)}, f32[1,512,512]{2,1,0:T(8,128)S(1)}, u32[]{:S(2)}) copy-start(f32[1,512,512]{2,1,0:T(8,128)S(1)} %convert_select_fusion) | copy-start | bytes 3145732
  449.6 4.1 copy-start.8
Sparse Core Ops, SparseCore 0:
  11.6 91.0 reduce-scatter.1
  456.5 381.3 all-gather.2
where the time goes:
time: 860 us; the launch traced here: 850 us
  waiting for transfers between devices  470 us (55%)
  other arithmetic  258 us (30%)
  matrix products  48.9 us (6%)
  local copies, waits for them, and re-layouts  40.2 us (5%)
  loops' own time  16.4 us (2%)
  between operations  16 us (2%)
    all_gather x1, waiting for transfers between devices, local(): lax.all_gather(outward.astype(jnp.bfloat16), 'replica', axis=0, tiled=True)  377 us
    another operation x29, other arithmetic, orthonormal(): lower_factor = jnp.linalg.cholesky(gram)  170 us
    reduce_scatter x1, waiting for transfers between devices, local(): lax.psum_scatter(gradients, 'replica', scatter_dimension=1, tiled=True)  91.6 us
    another operation x5, other arithmetic, orthonormal(): jax.scipy.linalg.solve_triangular(lower_factor, matrix.T, lower=True)  80.8 us
    another operation x27, local copies, waits for them, and re-layouts, orthonormal(): jax.scipy.linalg.solve_triangular(lower_factor, matrix.T, lower=True)  23 us
  transfers between devices with their start and end apart: 4, of which 3 were waited for; matrix products, arithmetic and copies ran while one was open for 2% of the time, Pallas kernels for 0%

commit v1 on v0

v1 whole, which is shorter than its diff:
```python
import functools

import jax
import jax.numpy as jnp
from jax import lax
from jax.experimental import pallas as pl
from jax.experimental.pallas import tpu as pltpu
from jax.sharding import PartitionSpec as P

POWER = 2


beta_one = 0.95
beta_two = 0.95
epsilon = 1e-08
bias_step = 10.0

TILE = 128
ROWS = 8


def paired(block):
    count = lax.axis_size("shard")
    return lax.ppermute(block, "shard", [(low, low ^ 1) for low in range(count)])


def product(left_side, right_side, contract=(1, 0), precision=lax.Precision.HIGHEST):
    return lax.dot_general(
        left_side,
        right_side,
        (((contract[0],), (contract[1],)), ((), ())),
        precision=precision,
        preferred_element_type=jnp.float32,
    )


def low_product(left_side, right_side, contract=(1, 0)):
    return product(
        left_side.astype(jnp.bfloat16), right_side.astype(jnp.bfloat16), contract, None
    )


def inverse_factor(tile):
    side = tile.shape[0]
    spread = (ROWS, side)
    lane = lax.broadcasted_iota(jnp.int32, spread, 1)
    sub = lax.broadcasted_iota(jnp.int32, spread, 0)
    count = side // ROWS
    groups = [tile[ROWS * g : ROWS * (g + 1), :] for g in range(count)]
    finished = []
    for step in range(count):
        start = ROWS * step
        head = groups[step]
        inside = (lane >= start) & (lane < start + ROWS)
        columns = [
            jnp.broadcast_to(head[:, start + j : start + j + 1], spread) for j in range(ROWS)
        ]
        small = [
            [jnp.broadcast_to(columns[j][i : i + 1, :], spread) for j in range(i + 1)]
            for i in range(ROWS)
        ]
        lines = [
            jnp.where(
                lane == start + i,
                1.0,
                jnp.where(inside, 0.0, jnp.broadcast_to(head[i : i + 1, :], spread)),
            )
            for i in range(ROWS)
        ]
        factor = [[None] * ROWS for _ in range(ROWS)]
        inverse = []
        for j in range(ROWS):
            inverse.append(1.0 / small[j][j])
            for i in range(j + 1, ROWS):
                factor[i][j] = small[i][j] * inverse[j]
            for i in range(j + 1, ROWS):
                lines[i] = lines[i] - factor[i][j] * lines[j]
                for t in range(j + 1, i + 1):
                    small[i][t] = small[i][t] - factor[i][j] * small[t][j]
        done = jnp.zeros(spread, jnp.float32)
        for j in range(ROWS):
            done = jnp.where(sub == j, lines[j] * lax.rsqrt(small[j][j]), done)
        finished.append(jnp.where(lane < start + ROWS, done, 0.0))
        if step + 1 == count:
            break
        back = [None] * ROWS
        for j in reversed(range(ROWS)):
            value = lines[j] * inverse[j]
            for i in reversed(range(j + 1, ROWS)):
                value = value - factor[i][j] * back[i]
            back[j] = value
        for g in range(step + 1, count):
            old = groups[g]
            terms = [
                jnp.broadcast_to(old[:, start + j : start + j + 1], spread) * back[j]
                for j in range(ROWS)
            ]
            while len(terms) > 1:
                terms = [terms[t] + terms[t + 1] for t in range(0, len(terms), 2)]
            groups[g] = jnp.where(inside, 0.0, old) - terms[0]
    return jnp.concatenate(finished, 0)


def refresh_kernel(factor_ref, turned_ref, out_ref, joint):
    side = factor_ref.shape[0]
    out_ref[...] = turned_ref[...].astype(jnp.float32)

    def repeat(_, carry):
        turned = product(out_ref[...].astype(jnp.bfloat16), factor_ref[...], precision=None)
        joint[:, side:] = turned
        joint[:, :side] = product(turned, turned, (1, 1))

        for block in range(side // TILE):
            at = block * TILE
            rows = pl.ds(at, TILE)
            inverse = inverse_factor(joint[rows, pl.ds(at, TILE)])
            fresh = product(inverse, joint[rows, side:])
            out_ref[rows, :] = fresh
            if at + TILE < side:
                rest = pl.ds(at + TILE, side - at - TILE)
                below = product(joint[rest, pl.ds(at, TILE)], inverse, (1, 1))
                joint[rest, rest] -= product(below, below, (1, 1))
                joint[rest, side:] -= product(below, fresh)
        return carry

    lax.fori_loop(0, POWER, repeat, 0)


def refresh(factor, turned):
    side = factor.shape[0]
    return pl.pallas_call(
        refresh_kernel,
        out_shape=jax.ShapeDtypeStruct((side, side), jnp.float32),
        in_specs=[pl.BlockSpec(memory_space=pltpu.VMEM)] * 2,
        out_specs=pl.BlockSpec(memory_space=pltpu.VMEM),
        scratch_shapes=[pltpu.VMEM((side, 2 * side), jnp.float32)],
        name="refresh",
    )(factor, turned)


def local(
    gradients,
    first_moment,
    second_moment,
    left_stat,
    right_stat,
    left_basis,
    right_basis,
    refresh_flags,
):
    replica_count = lax.axis_size("replica")
    owner_id = lax.axis_index("shard") * replica_count + lax.axis_index("replica")
    listed = lax.dynamic_index_in_dim(refresh_flags, owner_id, 0, keepdims=False) == 1
    moment, second = first_moment[0], second_moment[0]
    basis_left, basis_right = left_basis[0], right_basis[0]
    plain = low_product(low_product(basis_left, moment), basis_right, (1, 1))
    summed = lax.psum_scatter(gradients, "replica", scatter_dimension=1, tiled=True)[0, 0]
    low_grad = summed.astype(jnp.bfloat16)
    block_side = low_grad.shape[0]
    rate = (1.0 - beta_two) / block_side
    right_new = beta_two * right_stat[0] + rate * low_product(low_grad, low_grad, (0, 0))
    left_new = beta_two * left_stat[0] + rate * low_product(low_grad, low_grad, (1, 1))
    incoming = paired(jnp.stack([right_new, basis_right.T], 0).astype(jnp.bfloat16))
    chosen = jnp.where(
        listed, jnp.stack([left_new, basis_left.T], 0).astype(jnp.bfloat16), incoming
    )
    turned = refresh(chosen[0], chosen[1])
    arrived = paired(turned.astype(jnp.bfloat16))
    new_left = jnp.where(listed, turned.T, basis_left)
    new_right = jnp.where(listed, arrived.T.astype(jnp.float32), basis_right)
    both = jnp.concatenate([plain.astype(jnp.bfloat16), low_grad], 1)
    half = low_product(new_left, both, (0, 0))
    carried = jnp.where(listed, low_product(half[:, :block_side], new_right), moment)
    rotated = low_product(half[:, block_side:], new_right)
    moment_new = beta_one * carried + (1.0 - beta_one) * rotated
    second_new = beta_two * second + (1.0 - beta_two) * rotated * rotated
    scaled = (
        moment_new
        / (1.0 - beta_one**bias_step)
        / (jnp.sqrt(second_new / (1.0 - beta_two**bias_step)) + epsilon)
    )
    outward = low_product(low_product(new_left, scaled), new_right, (1, 1))
    gathered = lax.all_gather(outward.astype(jnp.bfloat16)[None], "replica", axis=0, tiled=True)
    return (
        gathered,
        moment_new[None],
        second_new[None],
        left_new[None],
        right_new[None],
        new_left[None],
        new_right[None],
    )


def solution(mesh):
    owned = P(("shard", "replica"), None, None)
    in_specs = (P("replica", "shard", None, None),) + (owned,) * 6 + (P(),)
    out_specs = (P("shard", None, None),) + (owned,) * 6
    return jax.shard_map(local, mesh=mesh, in_specs=in_specs, out_specs=out_specs, check_vma=False)
```

time: 860 us -> 276 us (0.32); the launches traced: 850 us -> 276 us
  waiting for transfers between devices: 470 us -> 150 us
  other arithmetic: 258 us -> 11.7 us
  Pallas kernels: 0 us -> 53.7 us
  matrix products: 48.9 us -> 13.8 us
  loops' own time: 16.4 us -> 0 us
  local copies, waits for them, and re-layouts: 40.2 us -> 31.2 us
    all_gather x1, waiting for transfers between devices: 377 us -> 56.3 us  [local(): lax.all_gather(outward.astype(jnp.bfloat16)[None], 'replica', axis=0, til...]
    another operation x36 -> x4, other arithmetic: 251 us -> 3.05 us  [the longest x2 1.92 us: local(): jnp.stack([left_new, basis_left.T], 0).astype(jnp.bfloat16)]
    pallas_call x0 -> x1, Pallas kernels: none -> 53.7 us  [refresh(): pl.pallas_call(refresh_kernel, out_shape=jax.ShapeDtypeStruct((side, side...]
    another operation x26 -> x0, matrix products: 24.1 us -> none  [the longest x14 13.2 us: orthonormal(): jax.scipy.linalg.solve_triangular(lower_factor, matrix.T, lower=True)]
    another operation x35 -> x2, local copies, waits for them, and re-layouts: 23.3 us -> 1.7 us  [the longest x1 1.49 us: local(): jnp.stack([left_new, basis_left.T], 0).astype(jnp.bfloat16)]
    unnamed x18 -> x43, local copies, waits for them, and re-layouts: 9.77 us -> 26.3 us
    another operation x5 -> x0, loops' own time: 16.4 us -> none  [the longest x1 9.25 us: local(): lax.cond(own_flags[position] == 1, lambda: power_step(left_new[position],...]
    dot_general x10 -> x7, matrix products: 24.8 us -> 13.8 us  [product(): lax.dot_general(left_side, right_side, (((contract[0],), (contract[1],)),...]
  transfers between devices with their start and end apart: 4 -> 4, of which waited for: 3 -> 2; matrix products, arithmetic and copies ran while one was open for 2% -> 12% of each run, Pallas kernels for 0% -> 0%
where the time goes in v1:
time: 276 us
  waiting for transfers between devices  150 us (54%)
  Pallas kernels  53.7 us (19%)
  local copies, waits for them, and re-layouts  31.2 us (11%)
  between operations  14.9 us (5%)
  matrix products  13.8 us (5%)
  other arithmetic  11.7 us (4%)
    reduce_scatter x1, waiting for transfers between devices, local(): lax.psum_scatter(gradients, 'replica', scatter_dimension=1, tiled=True)  93.1 us
    all_gather x1, waiting for transfers between devices, local(): lax.all_gather(outward.astype(jnp.bfloat16)[None], 'replica', axis=0, til...  56.3 us
    pallas_call x1, Pallas kernels, refresh(): pl.pallas_call(refresh_kernel, out_shape=jax.ShapeDtypeStruct((side, side...  53.7 us
    unnamed x43, local copies, waits for them, and re-layouts  26.3 us
    dot_general x7, matrix products, product(): lax.dot_general(left_side, right_side, (((contract[0],), (contract[1],)),...  13.8 us
  transfers between devices with their start and end apart: 4, of which 2 were waited for; matrix products, arithmetic and copies ran while one was open for 12% of the time, Pallas kernels for 0%

profile of v1, /device:TPU:0, one launch (start us, length us, event | category | flops | bytes accessed | tf_op | source)
XLA Modules:
  0.0 275.6 jit_solution(15276597166539757491)
XLA Ops:
  7.2 0.7 reduce-scatter.2.cloned.1.call-update
  9.6 93.1 %reduce-scatter.2.cloned.1.call-done = bf16[1,1,512,512]{3,2,1,0:T(8,128)(2,1)} async-done(((bf16[1,8,512,512]{3,2,1,0:T(8,128)(2,1)}), bf16[1,1,512,512]{3,2,1,0:T(8,128)(2,1)}) %reduce-scatter.2.cloned.1.call-update) | async-done | bytes 524304 | tf_op jit(solution)/shard_map/reduce_scatter | solution.py:157
  102.7 2.7 fusion.46
  105.7 1.1 pad_maximum_fusion.1
  106.7 2.6 copy.27
  109.3 2.6 copy.15
  112.0 1.3 copy.24
  113.3 0.6 dynamic_slice.4
  114.5 0.9 fusion.11
  115.4 1.5 convolution_convert_fusion.3
  116.9 3.1 %fusion.45 = (bf16[1,512,512]{1,2,0:T(8,128)(2,1)S(1)}, f32[1,512,512]{1,2,0:T(8,128)}) fusion(bf16[1,1,512,512]{3,2,1,0:T(8,128)(2,1)} %reduce-scatter.2.cloned.1.call-done, f32[1,512,512]{1,2,0:T(8,128)} %copy.15), kind=kOutput, calls=%fused_computation.52 | convolution fusion | flops 269484032 | bytes 3145728 | tf_op jit(solution)/shard_map/dot_general | solution.py:28
  120.0 1.1 pad_maximum_fusion
  121.0 1.5 copy.21
  122.5 1.3 broadcast_select_fusion
  123.9 1.0 slice_bitcast_fusion
  124.9 53.7 %refresh.1 = f32[512,512]{1,0:T(8,128)} custom-call(bf16[512,512]{1,0:T(8,128)(2,1)} %get-tuple-element.15.factor_ref, bf16[512,512]{1,0:T(8,128)(2,1)} %get-tuple-element.14.turned_ref), custom_call_target="tpu_custom_call" | custom-call | tf_op jit(solution)/shard_map/refresh/pallas_call | solution.py:131
  178.6 2.1 convert_element_type.57
  180.7 1.6 copy.22
  182.6 1.0 copy-done.10
  184.0 0.7 convolution_convert_fusion
  186.4 1.5 multiply_add_fusion
  187.9 3.8 %convolution_convert_fusion.1 = bf16[512,512]{1,0:T(8,128)(2,1)} fusion(bf16[512,512]{0,1:T(8,128)(2,1)} %copy-done.2, bf16[512,512]{1,0:T(8,128)(2,1)} %copy-done.14, f32[512,512]{0,1:T(8,128)} %multiply_add_fusion, f32[512,512]{0,1:T(8,128)S(1)} %fusion.12, f32[1,512,512]{1,2,0:T(8,128)} %copy.27), kind=kOutput, calls=%fused_computation.11 | convolution fusion | flops 539754496 | bytes 4718592 | tf_op jit(solution)/shard_map/dot_general | solution.py:28
  191.7 2.5 copy.31
  194.2 2.5 copy.32
  196.7 2.5 fusion.27
  199.2 1.1 fusion.9
  200.3 2.6 copy.33
  202.9 1.2 fusion.29
  204.1 2.5 copy.30
  206.6 1.3 copy.29
  207.9 56.3 %all-gather.3.cloned.1.call-done = bf16[4096,512]{1,0:T(8,128)(2,1)} async-done(((bf16[512,512]{1,0:T(8,128)(2,1)}), bf16[4096,512]{1,0:T(8,128)(2,1)}) %all-gather.3.cloned.1.call-update) | async-done | bytes 4194320 | tf_op jit(solution)/shard_map/all_gather | solution.py:183
  264.3 4.5 %copy.39 = bf16[8,512,512]{2,1,0:T(8,128)(2,1)} copy(bf16[8,512,512]{2,1,0:T(8,128)(2,1)} %bitcast.102) | data formatting | bytes 8388608
  (45 shorter events, 4.2 us)
Async XLA Ops:
  7.2 1.2 copy-start.11
  7.2 95.5 %reduce-scatter.2.cloned.1.call-start = ((), (), s32[]{:S(2)}) async-start(), calls=%async_computation.1 | async-start | bytes 4718592 | tf_op jit(solution)/shard_map/reduce_scatter | solution.py:157
  7.9 1.3 copy-start.12
  7.9 256.4 %all-gather.3.cloned.1.call-start = ((), (), s32[]{:S(2)}) async-start(), calls=%async_computation.2 | async-start | bytes 4718592 | tf_op jit(solution)/shard_map/all_gather | solution.py:183
  106.7 15.8 %collective-permute-start = (bf16[2,512,512]{2,1,0:T(8,128)(2,1)}, bf16[2,512,512]{2,1,0:T(8,128)(2,1)}, u32[]{:S(2)}, u32[]{:S(2)}) collective-permute-start(bf16[2,512,512]{2,1,0:T(8,128)(2,1)} %pad_maximum_fusion.1), channel_id=1, source_target_pairs={{0,8},{8,0},{16,24},{24,16},{1,9},{9,1},{17,25},{25,17},{2,10},{10... | collective-permute-start | bytes 3145736 | tf_op jit(solution)/shard_map/ppermute | solution.py:24
  106.7 5.2 %copy-start.3 = (f32[1,512,512]{2,1,0:T(8,128)S(1)}, f32[1,512,512]{2,1,0:T(8,128)}, u32[]{:S(2)}) copy-start(f32[1,512,512]{2,1,0:T(8,128)} %param.9) | copy-start | bytes 3145732
  109.3 3.9 %copy-start.15 = (s32[32]{0:T(128)S(1)}, s32[32]{0:T(128)}, u32[]{:S(2)}) copy-start(s32[32]{0:T(128)} %param.15) | copy-start | bytes 388
  109.3 5.2 %copy-start = (f32[1,512,512]{2,1,0:T(8,128)S(1)}, f32[1,512,512]{2,1,0:T(8,128)}, u32[]{:S(2)}) copy-start(f32[1,512,512]{2,1,0:T(8,128)} %param.13) | copy-start | bytes 3145732
  116.9 3.1 %copy-start.9 = (bf16[1,512,512]{1,2,0:T(8,128)(2,1)S(1)}, bf16[1,512,512]{1,2,0:T(8,128)(2,1)}, u32[]{:S(2)}) copy-start(bf16[1,512,512]{1,2,0:T(8,128)(2,1)} %fusion.11) | copy-start | bytes 1572868
  182.2 2.5 copy-start.1
  182.2 1.4 copy-start.10
  182.3 1.8 copy-start.13
  182.3 2.5 collective-permute-start.1
  182.6 2.4 copy-start.14
  184.8 1.6 copy-start.5
  184.8 0.8 copy-start.7
  185.0 0.8 copy-start.2
  196.7 2.5 copy-start.8
  199.2 3.7 %copy-start.4 = (f32[1,512,512]{1,2,0:T(8,128)S(1)}, f32[1,512,512]{1,2,0:T(8,128)}, u32[]{:S(2)}) copy-start(f32[1,512,512]{1,2,0:T(8,128)} %copy.27) | copy-start | bytes 3145732
  202.9 3.8 %copy-start.6 = (f32[512,512]{0,1:T(8,128)S(1)}, f32[512,512]{0,1:T(8,128)}, u32[]{:S(2)}) copy-start(f32[512,512]{0,1:T(8,128)} %multiply_add_fusion) | copy-start | bytes 3145732
Sparse Core Ops, SparseCore 0:
  11.6 91.0 reduce-scatter.1
  191.8 72.4 all-gather.2

commit v2 on v1

--- a/solution.py
+++ b/solution.py
@@ -1,5 +1,3 @@
-import functools
-
 import jax
 import jax.numpy as jnp
 from jax import lax
@@ -17,6 +15,8 @@
 
 TILE = 128
 ROWS = 8
+CHUNKS = 2
+MESH = pl.DeviceIdType.MESH
 
 
 def paired(block):
@@ -101,12 +101,27 @@
     return jnp.concatenate(finished, 0)
 
 
-def refresh_kernel(factor_ref, turned_ref, out_ref, joint):
-    side = factor_ref.shape[0]
-    out_ref[...] = turned_ref[...].astype(jnp.float32)
+def refresh_kernel(listed_ref, left_ref, left_basis_ref, incoming_ref, turned_ref, basis_ref, held, joint):
+    side = left_ref.shape[0]
+    listed = listed_ref[0] == 1
+
+    @pl.when(listed)
+    def _():
+        held[...] = left_basis_ref[...].T
+
+    @pl.when(jnp.logical_not(listed))
+    def _():
+        held[...] = incoming_ref[1].astype(jnp.float32).T
+
+    factor = jnp.where(
+        jnp.full((side, side), listed_ref[0], jnp.int32) == 1,
+        left_ref[...].astype(jnp.float32),
+        incoming_ref[0].astype(jnp.float32),
+    ).astype(jnp.bfloat16)
+    turned_ref[...] = factor
 
     def repeat(_, carry):
-        turned = product(out_ref[...].astype(jnp.bfloat16), factor_ref[...], precision=None)
+        turned = product(held[...].astype(jnp.bfloat16), turned_ref[...], precision=None)
         joint[:, side:] = turned
         joint[:, :side] = product(turned, turned, (1, 1))
 
@@ -115,7 +130,7 @@
             rows = pl.ds(at, TILE)
             inverse = inverse_factor(joint[rows, pl.ds(at, TILE)])
             fresh = product(inverse, joint[rows, side:])
-            out_ref[rows, :] = fresh
+            held[rows, :] = fresh
             if at + TILE < side:
                 rest = pl.ds(at + TILE, side - at - TILE)
                 below = product(joint[rest, pl.ds(at, TILE)], inverse, (1, 1))
@@ -124,18 +139,238 @@
         return carry
 
     lax.fori_loop(0, POWER, repeat, 0)
-
-
-def refresh(factor, turned):
-    side = factor.shape[0]
+    turned_ref[...] = held[...].T.astype(jnp.bfloat16)
+
+    @pl.when(listed)
+    def _():
+        basis_ref[...] = held[...].T
+
+    @pl.when(jnp.logical_not(listed))
+    def _():
+        basis_ref[...] = left_basis_ref[...]
+
+
+def statistics_kernel(grad_ref, left_ref, right_ref, basis_ref, left_out, right_out, low_out, send_out):
+    grad = grad_ref[...]
+    rate = (1.0 - beta_two) / grad.shape[0]
+    left = beta_two * left_ref[...] + rate * low_product(grad, grad, (1, 1))
+    left_out[...] = left
+    low_out[...] = left.astype(jnp.bfloat16)
+    right = beta_two * right_ref[...] + rate * low_product(grad, grad, (0, 0))
+    right_out[...] = right
+    send_out[0] = right.astype(jnp.bfloat16)
+    send_out[1] = basis_ref[...].astype(jnp.bfloat16)
+
+
+def update_kernel(
+    listed_ref,
+    grad_ref,
+    moment_ref,
+    second_ref,
+    old_left_ref,
+    old_right_ref,
+    left_ref,
+    arrived_ref,
+    moment_out,
+    second_out,
+    right_out,
+    direction_out,
+):
+    listed = listed_ref[0] == 1
+
+    @pl.when(listed)
+    def _():
+        right_out[...] = arrived_ref[...].astype(jnp.float32)
+        plain = low_product(
+            low_product(old_left_ref[...], moment_ref[...]), old_right_ref[...], (1, 1)
+        )
+        moment_out[...] = low_product(
+            low_product(left_ref[...], plain, (0, 0)), arrived_ref[...]
+        )
+
+    @pl.when(jnp.logical_not(listed))
+    def _():
+        right_out[...] = old_right_ref[...]
+        moment_out[...] = moment_ref[...]
+
+    left = left_ref[...].astype(jnp.bfloat16)
+    right = right_out[...].astype(jnp.bfloat16)
+    rotated = low_product(low_product(left, grad_ref[...], (0, 0)), right)
+    moment_new = beta_one * moment_out[...] + (1.0 - beta_one) * rotated
+    second_new = beta_two * second_ref[...] + (1.0 - beta_two) * rotated * rotated
+    moment_out[...] = moment_new
+    second_out[...] = second_new
+    scaled = (
+        moment_new
+        / (1.0 - beta_one**bias_step)
+        / (jnp.sqrt(second_new / (1.0 - beta_two**bias_step)) + epsilon)
+    )
+    direction_out[...] = low_product(low_product(left, scaled), right, (1, 1)).astype(
+        jnp.bfloat16
+    )
+
+
+def sequence(outer_count):
+    return sorted(range(outer_count), key=lambda m: (m == 0, abs(2 * m - outer_count), m))
+
+
+def place(outer_count):
+    me = lax.axis_index("replica")
+    inner = lax.rem(me, 2)
+    return me, inner, me // 2, me + 1 - 2 * inner
+
+
+def meet(outer_count):
+    me, inner, outer, partner = place(outer_count)
+    barrier = pltpu.get_barrier_semaphore()
+    pl.semaphore_signal(barrier, inc=1, device_id={"replica": partner}, device_id_type=MESH)
+    for m in range(1, outer_count):
+        other = lax.rem(outer + m, outer_count) * 2 + inner
+        pl.semaphore_signal(barrier, inc=1, device_id={"replica": other}, device_id_type=MESH)
+    pl.semaphore_wait(barrier, outer_count)
+
+
+def remote(source, target, send_sem, recv_sem, replica):
+    return pltpu.make_async_remote_copy(
+        src_ref=source,
+        dst_ref=target,
+        send_sem=send_sem,
+        recv_sem=recv_sem,
+        device_id={"replica": replica},
+        device_id_type=MESH,
+    )
+
+
+def sum_kernel(
+    grad_ref, out_ref, mine, got, pairs, far, load_sem, near_send, near_recv, far_send, far_recv
+):
+    outer_count = mine.shape[0]
+    rows = mine.shape[1] // CHUNKS
+    me, inner, outer, partner = place(outer_count)
+    meet(outer_count)
+    order = sequence(outer_count)
+    near, loads = {}, {}
+    for m in order:
+        aim = lax.rem(outer + m, outer_count)
+        for c in range(CHUNKS):
+            part = pl.ds(c * rows, rows)
+            near[m, c] = remote(
+                grad_ref.at[0, aim * 2 + 1 - inner, part],
+                got.at[m, part],
+                near_send.at[m, c],
+                near_recv.at[m, c],
+                partner,
+            )
+            near[m, c].start()
+        loads[m] = pltpu.make_async_copy(
+            grad_ref.at[0, aim * 2 + inner], mine.at[m], load_sem.at[m]
+        )
+        loads[m].start()
+    away = {}
+    for m in order:
+        aim = lax.rem(outer + m, outer_count)
+        loads[m].wait()
+        for c in range(CHUNKS):
+            part = pl.ds(c * rows, rows)
+            near[m, c].wait_recv()
+            total = mine[m, part].astype(jnp.float32) + got[m, part].astype(jnp.float32)
+            if m != 0:
+                pairs[m, part] = total.astype(jnp.bfloat16)
+                away[m, c] = remote(
+                    pairs.at[m, part],
+                    far.at[m, part],
+                    far_send.at[m, c],
+                    far_recv.at[m, c],
+                    aim * 2 + inner,
+                )
+                away[m, c].start()
+    for c in range(CHUNKS):
+        part = pl.ds(c * rows, rows)
+        total = mine[0, part].astype(jnp.float32) + got[0, part].astype(jnp.float32)
+        for m in order[:-1]:
+            away[m, c].wait_recv()
+            total = total + far[m, part].astype(jnp.float32)
+        out_ref[part] = total.astype(jnp.bfloat16)
+    for copy in list(near.values()) + list(away.values()):
+        copy.wait_send()
+
+
+def gather_kernel(block_ref, out_ref, own_sem, near_send, near_recv, far_send, far_recv):
+    outer_count = out_ref.shape[0] // 2
+    rows = block_ref.shape[0] // CHUNKS
+    me, inner, outer, partner = place(outer_count)
+    meet(outer_count)
+    order = sequence(outer_count)
+    keep = pltpu.make_async_copy(block_ref, out_ref.at[me], own_sem.at[0])
+    keep.start()
+    near, away = {}, {}
+    for m in order:
+        aim = lax.rem(outer + m, outer_count)
+        for c in range(CHUNKS):
+            part = pl.ds(c * rows, rows)
+            sems = (near_send, near_recv) if m == 0 else (far_send, far_recv)
+            copy = remote(
+                block_ref.at[part],
+                out_ref.at[me, part],
+                sems[0].at[m, c],
+                sems[1].at[m, c],
+                partner if m == 0 else aim * 2 + inner,
+            )
+            copy.start()
+            (near if m == 0 else away)[m, c] = copy
+    for c in range(CHUNKS):
+        for m in order[:-1]:
+            part = pl.ds(c * rows, rows)
+            source = lax.rem(outer + outer_count - m, outer_count) * 2 + inner
+            away[m, c].wait_recv()
+            near[m, c] = remote(
+                out_ref.at[source, part],
+                out_ref.at[source, part],
+                near_send.at[m, c],
+                near_recv.at[m, c],
+                partner,
+            )
+            near[m, c].start()
+    for copy in near.values():
+        copy.wait_recv()
+    for copy in list(near.values()) + list(away.values()):
+        copy.wait_send()
+    keep.wait()
+
+
+VMEM = pl.BlockSpec(memory_space=pltpu.VMEM)
+SMEM = pl.BlockSpec(memory_space=pltpu.SMEM)
+ANY = pl.BlockSpec(memory_space=pl.ANY)
+
+
+def replica_sum(gradients):
+    count, side = gradients.shape[1], gradients.shape[2]
+    outer = count // 2
+    held = pltpu.VMEM((outer, side, side), jnp.bfloat16)
+    flags = pltpu.SemaphoreType.DMA((outer, CHUNKS))
     return pl.pallas_call(
-        refresh_kernel,
-        out_shape=jax.ShapeDtypeStruct((side, side), jnp.float32),
-        in_specs=[pl.BlockSpec(memory_space=pltpu.VMEM)] * 2,
-        out_specs=pl.BlockSpec(memory_space=pltpu.VMEM),
-        scratch_shapes=[pltpu.VMEM((side, 2 * side), jnp.float32)],
-        name="refresh",
-    )(factor, turned)
+        sum_kernel,
+        out_shape=jax.ShapeDtypeStruct((side, side), jnp.bfloat16),
+        in_specs=[ANY],
+        out_specs=VMEM,
+        scratch_shapes=[held] * 4 + [pltpu.SemaphoreType.DMA((outer,))] + [flags] * 4,
+        compiler_params=pltpu.CompilerParams(collective_id=0, has_side_effects=True),
+        name="replica_sum",
+    )(gradients)
+
+
+def replica_gather(block, count):
+    side = block.shape[0]
+    flags = pltpu.SemaphoreType.DMA((count // 2, CHUNKS))
+    return pl.pallas_call(
+        gather_kernel,
+        out_shape=jax.ShapeDtypeStruct((count, side, side), jnp.bfloat16),
+        in_specs=[VMEM],
+        out_specs=ANY,
+        scratch_shapes=[pltpu.SemaphoreType.DMA((1,))] + [flags] * 4,
+        compiler_params=pltpu.CompilerParams(collective_id=1, has_side_effects=True),
+        name="replica_gather",
+    )(block)
 
 
 def local(
@@ -150,37 +385,48 @@
 ):
     replica_count = lax.axis_size("replica")
     owner_id = lax.axis_index("shard") * replica_count + lax.axis_index("replica")
-    listed = lax.dynamic_index_in_dim(refresh_flags, owner_id, 0, keepdims=False) == 1
-    moment, second = first_moment[0], second_moment[0]
-    basis_left, basis_right = left_basis[0], right_basis[0]
-    plain = low_product(low_product(basis_left, moment), basis_right, (1, 1))
-    summed = lax.psum_scatter(gradients, "replica", scatter_dimension=1, tiled=True)[0, 0]
-    low_grad = summed.astype(jnp.bfloat16)
-    block_side = low_grad.shape[0]
-    rate = (1.0 - beta_two) / block_side
-    right_new = beta_two * right_stat[0] + rate * low_product(low_grad, low_grad, (0, 0))
-    left_new = beta_two * left_stat[0] + rate * low_product(low_grad, low_grad, (1, 1))
-    incoming = paired(jnp.stack([right_new, basis_right.T], 0).astype(jnp.bfloat16))
-    chosen = jnp.where(
-        listed, jnp.stack([left_new, basis_left.T], 0).astype(jnp.bfloat16), incoming
-    )
-    turned = refresh(chosen[0], chosen[1])
-    arrived = paired(turned.astype(jnp.bfloat16))
-    new_left = jnp.where(listed, turned.T, basis_left)
-    new_right = jnp.where(listed, arrived.T.astype(jnp.float32), basis_right)
-    both = jnp.concatenate([plain.astype(jnp.bfloat16), low_grad], 1)
-    half = low_product(new_left, both, (0, 0))
-    carried = jnp.where(listed, low_product(half[:, :block_side], new_right), moment)
-    rotated = low_product(half[:, block_side:], new_right)
-    moment_new = beta_one * carried + (1.0 - beta_one) * rotated
-    second_new = beta_two * second + (1.0 - beta_two) * rotated * rotated
-    scaled = (
-        moment_new
-        / (1.0 - beta_one**bias_step)
-        / (jnp.sqrt(second_new / (1.0 - beta_two**bias_step)) + epsilon)
-    )
-    outward = low_product(low_product(new_left, scaled), new_right, (1, 1))
-    gathered = lax.all_gather(outward.astype(jnp.bfloat16)[None], "replica", axis=0, tiled=True)
+    listed = lax.dynamic_slice_in_dim(refresh_flags, owner_id, 1)
+    side = left_stat.shape[1]
+    wide = jax.ShapeDtypeStruct((side, side), jnp.float32)
+    low = jax.ShapeDtypeStruct((side, side), jnp.bfloat16)
+    low_grad = replica_sum(gradients)
+    left_new, right_new, left_low, outgoing = pl.pallas_call(
+        statistics_kernel,
+        out_shape=(wide, wide, low, jax.ShapeDtypeStruct((2, side, side), jnp.bfloat16)),
+        in_specs=[VMEM] * 4,
+        out_specs=(VMEM,) * 4,
+        name="statistics",
+    )(low_grad, left_stat[0], right_stat[0], right_basis[0])
+    incoming = paired(outgoing)
+    turned, new_left = pl.pallas_call(
+        refresh_kernel,
+        out_shape=(low, wide),
+        in_specs=[SMEM] + [VMEM] * 3,
+        out_specs=(VMEM,) * 2,
+        scratch_shapes=[
+            pltpu.VMEM((side, side), jnp.float32),
+            pltpu.VMEM((side, 2 * side), jnp.float32),
+        ],
+        name="refresh",
+    )(listed, left_low, left_basis[0], incoming)
+    arrived = paired(turned)
+    moment_new, second_new, new_right, outward = pl.pallas_call(
+        update_kernel,
+        out_shape=(wide, wide, wide, low),
+        in_specs=[SMEM] + [VMEM] * 7,
+        out_specs=(VMEM,) * 4,
+        name="update",
+    )(
+        listed,
+        low_grad,
+        first_moment[0],
+        second_moment[0],
+        left_basis[0],
+        right_basis[0],
+        new_left,
+        arrived,
+    )
+    gathered = replica_gather(outward, replica_count)
     return (
         gathered,
         moment_new[None],

time: 276 us -> 210 us (0.76)
  waiting for transfers between devices: 150 us -> 4.01 us
  Pallas kernels: 53.7 us -> 196 us
  local copies, waits for them, and re-layouts: 31.2 us -> 6.83 us
  between operations: 14.9 us -> 0.66 us
  matrix products: 13.8 us -> 0 us
  other arithmetic: 11.7 us -> 0 us
    pallas_call x1 -> x5, Pallas kernels: 53.7 us -> 196 us  [the longest x1 69.9 us: replica_gather(): pl.pallas_call(gather_kernel, out_shape=jax.ShapeDtypeStruct((count, side...]
    reduce_scatter x1 -> x0, waiting for transfers between devices: 93.1 us -> none  [local(): lax.psum_scatter(gradients, 'replica', scatter_dimension=1, tiled=True)]
    all_gather x1 -> x0, waiting for transfers between devices: 56.3 us -> none  [local(): lax.all_gather(outward.astype(jnp.bfloat16)[None], 'replica', axis=0, til...]
    unnamed x43 -> x7, local copies, waits for them, and re-layouts: 26.3 us -> 6.24 us
    dot_general x7 -> x0, matrix products: 13.8 us -> none  [product(): lax.dot_general(left_side, right_side, (((contract[0],), (contract[1],)),...]
    broadcast_in_dim x3 -> x0, other arithmetic: 4.8 us -> none  [the longest x1 2.46 us: local(): new_left[None]]
    ppermute x2, waiting for transfers between devices: 0.01 us -> 4.01 us  [paired(): lax.ppermute(block, 'shard', [(low, low ^ 1) for low in range(count)])]
    another operation x4 -> x0, other arithmetic: 3.05 us -> none  [the longest x2 1.92 us: local(): jnp.stack([left_new, basis_left.T], 0).astype(jnp.bfloat16)]
  transfers between devices with their start and end apart: 4 -> 2, of which waited for: 2 -> 2; matrix products, arithmetic and copies ran while one was open for 12% -> 0% of each run, Pallas kernels for 0% -> 0%
where the time goes in v2:
time: 210 us; the launch traced here: 208 us
  Pallas kernels  196 us (93%)
  local copies, waits for them, and re-layouts  6.83 us (3%)
  waiting for transfers between devices  4.01 us (2%)
    pallas_call x1, Pallas kernels, replica_gather(): pl.pallas_call(gather_kernel, out_shape=jax.ShapeDtypeStruct((count, side...  69.9 us
    pallas_call x1, Pallas kernels, replica_sum(): pl.pallas_call(sum_kernel, out_shape=jax.ShapeDtypeStruct((side, side), j...  59.4 us
    pallas_call x1, Pallas kernels, local(): pl.pallas_call(refresh_kernel, out_shape=(low, wide), in_specs=[SMEM] + [...  55.5 us
    pallas_call x1, Pallas kernels, local(): pl.pallas_call(update_kernel, out_shape=(wide, wide, wide, low), in_specs...  6.78 us
    unnamed x7, local copies, waits for them, and re-layouts  6.24 us
    pallas_call x1, Pallas kernels, local(): pl.pallas_call(statistics_kernel, out_shape=(wide, wide, low, jax.ShapeDt...  4.38 us
  transfers between devices with their start and end apart: 2, of which 2 were waited for; matrix products, arithmetic and copies ran while one was open for 0% of the time, Pallas kernels for 0%

profile of v2, /device:TPU:0, one launch (start us, length us, event | category | flops | bytes accessed | tf_op | source)
XLA Modules:
  0.0 208.0 jit_solution(2862597243639483824)
XLA Ops:
  0.6 0.0 copy-start.2
  0.6 59.4 %replica_sum.1.grad_ref = bf16[512,512]{1,0:T(8,128)(2,1)} custom-call(bf16[1,8,512,512]{3,2,1,0:T(8,128)(2,1)} %grad_ref.1), custom_call_target="tpu_custom_call" | custom-call | tf_op jit(solution)/shard_map/replica_sum/pallas_call | solution.py:351
  60.0 4.4 %statistics.1 = (f32[512,512]{1,0:T(8,128)}, f32[512,512]{1,0:T(8,128)}, bf16[512,512]{1,0:T(8,128)(2,1)}, bf16[2,512,512]{2,1,0:T(8,128)(2,1)}) custom-call(bf16[512,512]{1,0:T(8,128)(2,1)} %replica_sum.1.grad_ref, f32[512,512]{1,0:T(8,128)} %bitcast.16, f32[512,512]{1,0:T(8,128)} %bitcast.17, f32[512,512]{1,0:T(8,128)} %bitcast.12), custom_call_target="tpu_custom_call" | custom-call | tf_op jit(solution)/shard_map/statistics/pallas_call | solution.py:393
  64.4 0.0 collective-permute-start
  64.4 0.0 copy-done.2
  64.4 0.6 dynamic_slice.3.listed_ref
  65.0 2.3 %collective-permute-done.incoming_ref = bf16[2,512,512]{2,1,0:T(8,128)(2,1)S(1)} collective-permute-done((bf16[2,512,512]{2,1,0:T(8,128)(2,1)}, bf16[2,512,512]{2,1,0:T(8,128)(2,1)S(1)}, u32[]{:S(2)}, u32[]{:S(2)}) %collective-permute-start) | collective-permute-done | bytes 1048608 | tf_op jit(solution)/shard_map/ppermute | solution.py:24
  67.3 0.0 copy-start
  67.3 1.0 copy-done
  68.2 55.5 %refresh.1 = (bf16[512,512]{1,0:T(8,128)(2,1)}, f32[512,512]{1,0:T(8,128)}) custom-call(s32[1]{0:T(128)} %dynamic_slice.3.listed_ref, bf16[512,512]{1,0:T(8,128)(2,1)} %get-tuple-element.17.left_ref, f32[512,512]{1,0:T(8,128)} %bitcast.14, bf16[2,512,512]{2,1,0:T(8,128)(2,1)} %copy-done), custom_call_target="tpu_custom_call" | custom-call | tf_op jit(solution)/shard_map/refresh/pallas_call | solution.py:401
  123.7 0.5 collective-permute-start.1
  124.2 1.7 collective-permute-done.1.arrived_ref
  126.0 0.0 copy-start.1
  126.0 0.8 copy-done.1
  126.8 6.8 %update.1 = (f32[512,512]{1,0:T(8,128)}, f32[512,512]{1,0:T(8,128)}, f32[512,512]{1,0:T(8,128)}, bf16[512,512]{1,0:T(8,128)(2,1)}) custom-call(s32[1]{0:T(128)} %dynamic_slice.3.listed_ref, bf16[512,512]{1,0:T(8,128)(2,1)} %replica_sum.1.grad_ref, f32[512,512]{1,0:T(8,128)} %bitcast.18, f32[512,512]{1,0:T(8,128)} %bitcast.19, f32[512,512]{1,0:T(8,128)} %bitcast.15, ...), custom_call_target="tpu_custom_call" | custom-call | tf_op jit(solution)/shard_map/update/pallas_call | solution.py:413
  133.6 69.9 %replica_gather.1 = bf16[8,512,512]{2,1,0:T(8,128)(2,1)} custom-call(bf16[512,512]{1,0:T(8,128)(2,1)} %get-tuple-element.21.block_ref), custom_call_target="tpu_custom_call" | custom-call | tf_op jit(solution)/shard_map/replica_gather/pallas_call | solution.py:365
  203.5 4.5 %copy.16 = bf16[8,512,512]{2,1,0:T(8,128)(2,1)} copy(bf16[8,512,512]{2,1,0:T(8,128)(2,1)} %replica_gather.1) | data formatting | bytes 8388608
Async XLA Ops:
  0.6 63.8 %copy-start.2 = (s32[32]{0:T(128)S(1)}, s32[32]{0:T(128)}, u32[]{:S(2)}) copy-start(s32[32]{0:T(128)} %param.15) | copy-start | bytes 388
  64.4 2.9 %collective-permute-start = (bf16[2,512,512]{2,1,0:T(8,128)(2,1)}, bf16[2,512,512]{2,1,0:T(8,128)(2,1)S(1)}, u32[]{:S(2)}, u32[]{:S(2)}) collective-permute-start(bf16[2,512,512]{2,1,0:T(8,128)(2,1)} %get-tuple-element.18), channel_id=1, source_target_pairs={{0,8},{8,0},{16,24},{24,16},{1,9},{9,1},{17,25},{25,17},{2,10},{10... | collective-permute-start | bytes 3145736 | tf_op jit(solution)/shard_map/ppermute | solution.py:24
  67.3 1.0 copy-start
  123.7 2.3 %collective-permute-start.1 = (bf16[512,512]{1,0:T(8,128)(2,1)}, bf16[512,512]{1,0:T(8,128)(2,1)S(1)}, u32[]{:S(2)}, u32[]{:S(2)}) collective-permute-start(bf16[512,512]{1,0:T(8,128)(2,1)} %get-tuple-element.20), channel_id=1, source_target_pairs={{0,8},{8,0},{16,24},{24,16},{1,9},{9,1},{17,25},{25,17},{2,10},{10... | collective-permute-start | bytes 1572872 | tf_op jit(solution)/shard_map/ppermute | solution.py:24
  126.0 0.8 copy-start.1

commit v3 on v2

--- a/solution.py
+++ b/solution.py
@@ -15,7 +15,7 @@
 
 TILE = 128
 ROWS = 8
-CHUNKS = 2
+CHUNKS = 4
 MESH = pl.DeviceIdType.MESH
 
 
@@ -125,17 +125,24 @@
         joint[:, side:] = turned
         joint[:, :side] = product(turned, turned, (1, 1))
 
+        tile = joint[:TILE, :TILE]
         for block in range(side // TILE):
-            at = block * TILE
-            rows = pl.ds(at, TILE)
-            inverse = inverse_factor(joint[rows, pl.ds(at, TILE)])
-            fresh = product(inverse, joint[rows, side:])
-            held[rows, :] = fresh
-            if at + TILE < side:
-                rest = pl.ds(at + TILE, side - at - TILE)
-                below = product(joint[rest, pl.ds(at, TILE)], inverse, (1, 1))
-                joint[rest, rest] -= product(below, below, (1, 1))
-                joint[rest, side:] -= product(below, fresh)
+            at, after = block * TILE, (block + 1) * TILE
+            inverse = inverse_factor(tile)
+            if after < side:
+                near = product(joint[after : after + TILE, at:after], inverse, (1, 1))
+                tile = joint[after : after + TILE, after : after + TILE] - product(
+                    near, near, (1, 1)
+                )
+            fresh = product(inverse, joint[at:after, side:])
+            held[at:after, :] = fresh
+            if after < side:
+                joint[after : after + TILE, side:] -= product(near, fresh)
+            if after + TILE < side:
+                below = product(joint[after + TILE :, at:after], inverse, (1, 1))
+                joint[after + TILE :, after : after + TILE] -= product(below, near, (1, 1))
+                joint[after + TILE :, after + TILE : side] -= product(below, below, (1, 1))
+                joint[after + TILE :, side:] -= product(below, fresh)
         return carry
 
     lax.fori_loop(0, POWER, repeat, 0)
@@ -295,46 +302,70 @@
         copy.wait_send()
 
 
-def gather_kernel(block_ref, out_ref, own_sem, near_send, near_recv, far_send, far_recv):
+def gather_kernel(
+    block_ref, out_ref, own_sem, near_send, near_recv, up_send, up_recv, down_send, down_recv
+):
     outer_count = out_ref.shape[0] // 2
     rows = block_ref.shape[0] // CHUNKS
     me, inner, outer, partner = place(outer_count)
     meet(outer_count)
-    order = sequence(outer_count)
     keep = pltpu.make_async_copy(block_ref, out_ref.at[me], own_sem.at[0])
     keep.start()
-    near, away = {}, {}
-    for m in order:
-        aim = lax.rem(outer + m, outer_count)
+
+    def above():
+        return outer + 1 < outer_count
+
+    def below():
+        return outer >= 1
+
+    def move(kind, distance, c):
+        part = pl.ds(c * rows, rows)
+        if kind == "up":
+            sems, target, origin = (up_send, up_recv), me + 2, me - 2 * distance
+        elif kind == "down":
+            sems, target, origin = (down_send, down_recv), me - 2, me + 2 * distance
+        else:
+            sems, target, origin = (near_send, near_recv), partner, me + 2 * distance
+        slot = distance + outer_count - 1 if kind == "near" else distance
+        source = block_ref.at[part] if distance == 0 else out_ref.at[origin, part]
+        return remote(
+            source, out_ref.at[origin, part], sems[0].at[slot, c], sems[1].at[slot, c], target
+        )
+
+    for c in range(CHUNKS):
+        pl.when(above())(move("up", 0, c).start)
+        pl.when(below())(move("down", 0, c).start)
+    for c in range(CHUNKS):
+        move("near", 0, c).start()
+    for distance in range(1, outer_count):
         for c in range(CHUNKS):
-            part = pl.ds(c * rows, rows)
-            sems = (near_send, near_recv) if m == 0 else (far_send, far_recv)
-            copy = remote(
-                block_ref.at[part],
-                out_ref.at[me, part],
-                sems[0].at[m, c],
-                sems[1].at[m, c],
-                partner if m == 0 else aim * 2 + inner,
-            )
-            copy.start()
-            (near if m == 0 else away)[m, c] = copy
-    for c in range(CHUNKS):
-        for m in order[:-1]:
-            part = pl.ds(c * rows, rows)
-            source = lax.rem(outer + outer_count - m, outer_count) * 2 + inner
-            away[m, c].wait_recv()
-            near[m, c] = remote(
-                out_ref.at[source, part],
-                out_ref.at[source, part],
-                near_send.at[m, c],
-                near_recv.at[m, c],
-                partner,
-            )
-            near[m, c].start()
-    for copy in near.values():
-        copy.wait_recv()
-    for copy in list(near.values()) + list(away.values()):
-        copy.wait_send()
+
+            @pl.when(outer >= distance)
+            def _():
+                move("up", distance - 1, c).wait_recv()
+                pl.when(above())(move("up", distance, c).start)
+                move("near", -distance, c).start()
+
+            @pl.when(outer + distance < outer_count)
+            def _():
+                move("down", distance - 1, c).wait_recv()
+                pl.when(below())(move("down", distance, c).start)
+                move("near", distance, c).start()
+
+    for distance in range(outer_count):
+        for c in range(CHUNKS):
+
+            @pl.when(outer >= distance)
+            def _():
+                move("near", -distance, c).wait()
+                pl.when(above())(move("up", distance, c).wait_send)
+
+            @pl.when(outer + distance < outer_count)
+            def _():
+                if distance:
+                    move("near", distance, c).wait()
+                pl.when(below())(move("down", distance, c).wait_send)
+
     keep.wait()
 
 
@@ -361,13 +392,15 @@
 
 def replica_gather(block, count):
     side = block.shape[0]
-    flags = pltpu.SemaphoreType.DMA((count // 2, CHUNKS))
+    outer = count // 2
+    flags = pltpu.SemaphoreType.DMA((outer, CHUNKS))
+    wide = pltpu.SemaphoreType.DMA((2 * outer - 1, CHUNKS))
     return pl.pallas_call(
         gather_kernel,
         out_shape=jax.ShapeDtypeStruct((count, side, side), jnp.bfloat16),
         in_specs=[VMEM],
         out_specs=ANY,
-        scratch_shapes=[pltpu.SemaphoreType.DMA((1,))] + [flags] * 4,
+        scratch_shapes=[pltpu.SemaphoreType.DMA((1,))] + [wide] * 2 + [flags] * 4,
         compiler_params=pltpu.CompilerParams(collective_id=1, has_side_effects=True),
         name="replica_gather",
     )(block)

time: 210 us -> 185 us (0.88)
  Pallas kernels: 196 us -> 172 us
    pallas_call x1, Pallas kernels: 69.9 us -> 48.7 us  [replica_gather(): pl.pallas_call(gather_kernel, out_shape=jax.ShapeDtypeStruct((count, side...]
    pallas_call x1, Pallas kernels: 59.4 us -> 56.8 us  [replica_sum(): pl.pallas_call(sum_kernel, out_shape=jax.ShapeDtypeStruct((side, side), j...]
where the time goes in v3:
time: 185 us; the launch traced here: 184 us
  Pallas kernels  172 us (93%)
  local copies, waits for them, and re-layouts  6.83 us (4%)
  waiting for transfers between devices  4.37 us (2%)
    pallas_call x1, Pallas kernels, replica_sum(): pl.pallas_call(sum_kernel, out_shape=jax.ShapeDtypeStruct((side, side), j...  56.8 us
    pallas_call x1, Pallas kernels, local(): pl.pallas_call(refresh_kernel, out_shape=(low, wide), in_specs=[SMEM] + [...  54.4 us
    pallas_call x1, Pallas kernels, replica_gather(): pl.pallas_call(gather_kernel, out_shape=jax.ShapeDtypeStruct((count, side...  48.7 us
    pallas_call x1, Pallas kernels, local(): pl.pallas_call(update_kernel, out_shape=(wide, wide, wide, low), in_specs...  8.05 us
    unnamed x7, local copies, waits for them, and re-layouts  6.24 us
    ppermute x2, waiting for transfers between devices, paired(): lax.ppermute(block, 'shard', [(low, low ^ 1) for low in range(count)])  4.37 us
    pallas_call x1, Pallas kernels, local(): pl.pallas_call(statistics_kernel, out_shape=(wide, wide, low, jax.ShapeDt...  4.36 us
  transfers between devices with their start and end apart: 2, of which 2 were waited for; matrix products, arithmetic and copies ran while one was open for 0% of the time, Pallas kernels for 0%

profile of v3, /device:TPU:0, one launch (start us, length us, event | category | flops | bytes accessed | tf_op | source)
XLA Modules:
  0.0 184.3 jit_solution(4881320660545138468)
XLA Ops:
  0.6 0.0 copy-start.2
  0.6 56.8 %replica_sum.1.grad_ref = bf16[512,512]{1,0:T(8,128)(2,1)} custom-call(bf16[1,8,512,512]{3,2,1,0:T(8,128)(2,1)} %grad_ref.1), custom_call_target="tpu_custom_call" | custom-call | tf_op jit(solution)/shard_map/replica_sum/pallas_call | solution.py:382
  57.5 4.4 %statistics.1 = (f32[512,512]{1,0:T(8,128)}, f32[512,512]{1,0:T(8,128)}, bf16[512,512]{1,0:T(8,128)(2,1)}, bf16[2,512,512]{2,1,0:T(8,128)(2,1)}) custom-call(bf16[512,512]{1,0:T(8,128)(2,1)} %replica_sum.1.grad_ref, f32[512,512]{1,0:T(8,128)} %bitcast.16, f32[512,512]{1,0:T(8,128)} %bitcast.17, f32[512,512]{1,0:T(8,128)} %bitcast.12), custom_call_target="tpu_custom_call" | custom-call | tf_op jit(solution)/shard_map/statistics/pallas_call | solution.py:426
  61.8 0.0 collective-permute-start
  61.9 0.0 copy-done.2
  61.9 0.6 dynamic_slice.3.listed_ref
  62.5 2.2 %collective-permute-done.incoming_ref = bf16[2,512,512]{2,1,0:T(8,128)(2,1)S(1)} collective-permute-done((bf16[2,512,512]{2,1,0:T(8,128)(2,1)}, bf16[2,512,512]{2,1,0:T(8,128)(2,1)S(1)}, u32[]{:S(2)}, u32[]{:S(2)}) %collective-permute-start) | collective-permute-done | bytes 1048608 | tf_op jit(solution)/shard_map/ppermute | solution.py:24
  64.7 0.0 copy-start
  64.7 1.0 copy-done
  65.7 54.4 %refresh.1 = (bf16[512,512]{1,0:T(8,128)(2,1)}, f32[512,512]{1,0:T(8,128)}) custom-call(s32[1]{0:T(128)} %dynamic_slice.3.listed_ref, bf16[512,512]{1,0:T(8,128)(2,1)} %get-tuple-element.17.left_ref, f32[512,512]{1,0:T(8,128)} %bitcast.14, bf16[2,512,512]{2,1,0:T(8,128)(2,1)} %copy-done), custom_call_target="tpu_custom_call" | custom-call | tf_op jit(solution)/shard_map/refresh/pallas_call | solution.py:434
  120.1 0.0 collective-permute-start.1
  120.1 2.1 %collective-permute-done.1.arrived_ref = bf16[512,512]{1,0:T(8,128)(2,1)S(1)} collective-permute-done((bf16[512,512]{1,0:T(8,128)(2,1)}, bf16[512,512]{1,0:T(8,128)(2,1)S(1)}, u32[]{:S(2)}, u32[]{:S(2)}) %collective-permute-start.1) | collective-permute-done | bytes 524320 | tf_op jit(solution)/shard_map/ppermute | solution.py:24
  122.2 0.0 copy-start.1
  122.2 0.8 copy-done.1
  123.0 8.0 %update.1 = (f32[512,512]{1,0:T(8,128)}, f32[512,512]{1,0:T(8,128)}, f32[512,512]{1,0:T(8,128)}, bf16[512,512]{1,0:T(8,128)(2,1)}) custom-call(s32[1]{0:T(128)} %dynamic_slice.3.listed_ref, bf16[512,512]{1,0:T(8,128)(2,1)} %replica_sum.1.grad_ref, f32[512,512]{1,0:T(8,128)} %bitcast.18, f32[512,512]{1,0:T(8,128)} %bitcast.19, f32[512,512]{1,0:T(8,128)} %bitcast.15, ...), custom_call_target="tpu_custom_call" | custom-call | tf_op jit(solution)/shard_map/update/pallas_call | solution.py:446
  131.0 48.7 %replica_gather.1 = bf16[8,512,512]{2,1,0:T(8,128)(2,1)} custom-call(bf16[512,512]{1,0:T(8,128)(2,1)} %get-tuple-element.21.block_ref), custom_call_target="tpu_custom_call" | custom-call | tf_op jit(solution)/shard_map/replica_gather/pallas_call | solution.py:398
  179.8 4.5 %copy.16 = bf16[8,512,512]{2,1,0:T(8,128)(2,1)} copy(bf16[8,512,512]{2,1,0:T(8,128)(2,1)} %replica_gather.1) | data formatting | bytes 8388608
Async XLA Ops:
  0.6 61.2 %copy-start.2 = (s32[32]{0:T(128)S(1)}, s32[32]{0:T(128)}, u32[]{:S(2)}) copy-start(s32[32]{0:T(128)} %param.15) | copy-start | bytes 388
  61.8 2.9 %collective-permute-start = (bf16[2,512,512]{2,1,0:T(8,128)(2,1)}, bf16[2,512,512]{2,1,0:T(8,128)(2,1)S(1)}, u32[]{:S(2)}, u32[]{:S(2)}) collective-permute-start(bf16[2,512,512]{2,1,0:T(8,128)(2,1)} %get-tuple-element.18), channel_id=1, source_target_pairs={{0,8},{8,0},{16,24},{24,16},{1,9},{9,1},{17,25},{25,17},{2,10},{10... | collective-permute-start | bytes 3145736 | tf_op jit(solution)/shard_map/ppermute | solution.py:24
  64.7 1.0 copy-start
  120.1 2.1 %collective-permute-start.1 = (bf16[512,512]{1,0:T(8,128)(2,1)}, bf16[512,512]{1,0:T(8,128)(2,1)S(1)}, u32[]{:S(2)}, u32[]{:S(2)}) collective-permute-start(bf16[512,512]{1,0:T(8,128)(2,1)} %get-tuple-element.20), channel_id=1, source_target_pairs={{0,8},{8,0},{16,24},{24,16},{1,9},{9,1},{17,25},{25,17},{2,10},{10... | collective-permute-start | bytes 1572872 | tf_op jit(solution)/shard_map/ppermute | solution.py:24
  122.2 0.8 copy-start.1

commit v4 on v3

--- a/solution.py
+++ b/solution.py
@@ -15,7 +15,7 @@
 
 TILE = 128
 ROWS = 8
-CHUNKS = 4
+CHUNKS = 8
 MESH = pl.DeviceIdType.MESH
 
 
@@ -123,7 +123,8 @@
     def repeat(_, carry):
         turned = product(held[...].astype(jnp.bfloat16), turned_ref[...], precision=None)
         joint[:, side:] = turned
-        joint[:, :side] = product(turned, turned, (1, 1))
+        for at in range(0, side, TILE):
+            joint[at:, at : at + TILE] = product(turned[at:], turned[at : at + TILE], (1, 1))
 
         tile = joint[:TILE, :TILE]
         for block in range(side // TILE):

time: 185 us -> 186 us (level)
  Pallas kernels: 172 us -> 174 us
    pallas_call x1, Pallas kernels: 48.7 us -> 51.2 us  [replica_gather(): pl.pallas_call(gather_kernel, out_shape=jax.ShapeDtypeStruct((count, side...]
where the time goes in v4:
time: 186 us
  Pallas kernels  174 us (94%)
  local copies, waits for them, and re-layouts  6.83 us (4%)
  waiting for transfers between devices  4.38 us (2%)
    pallas_call x1, Pallas kernels, replica_sum(): pl.pallas_call(sum_kernel, out_shape=jax.ShapeDtypeStruct((side, side), j...  56.2 us
    pallas_call x1, Pallas kernels, local(): pl.pallas_call(refresh_kernel, out_shape=(low, wide), in_specs=[SMEM] + [...  54.3 us
    pallas_call x1, Pallas kernels, replica_gather(): pl.pallas_call(gather_kernel, out_shape=jax.ShapeDtypeStruct((count, side...  51.2 us
    pallas_call x1, Pallas kernels, local(): pl.pallas_call(update_kernel, out_shape=(wide, wide, wide, low), in_specs...  8.05 us
    unnamed x7, local copies, waits for them, and re-layouts  6.24 us
    ppermute x2, waiting for transfers between devices, paired(): lax.ppermute(block, 'shard', [(low, low ^ 1) for low in range(count)])  4.38 us
    pallas_call x1, Pallas kernels, local(): pl.pallas_call(statistics_kernel, out_shape=(wide, wide, low, jax.ShapeDt...  4.38 us
  transfers between devices with their start and end apart: 2, of which 2 were waited for; matrix products, arithmetic and copies ran while one was open for 0% of the time, Pallas kernels for 0%

profile of v4, /device:TPU:0, one launch (start us, length us, event | category | flops | bytes accessed | tf_op | source)
XLA Modules:
  0.0 186.0 jit_solution(4112716721938681462)
XLA Ops:
  0.6 0.0 copy-start.2
  0.6 56.2 %replica_sum.1.grad_ref = bf16[512,512]{1,0:T(8,128)(2,1)} custom-call(bf16[1,8,512,512]{3,2,1,0:T(8,128)(2,1)} %grad_ref.1), custom_call_target="tpu_custom_call" | custom-call | tf_op jit(solution)/shard_map/replica_sum/pallas_call | solution.py:383
  56.8 4.4 %statistics.1 = (f32[512,512]{1,0:T(8,128)}, f32[512,512]{1,0:T(8,128)}, bf16[512,512]{1,0:T(8,128)(2,1)}, bf16[2,512,512]{2,1,0:T(8,128)(2,1)}) custom-call(bf16[512,512]{1,0:T(8,128)(2,1)} %replica_sum.1.grad_ref, f32[512,512]{1,0:T(8,128)} %bitcast.16, f32[512,512]{1,0:T(8,128)} %bitcast.17, f32[512,512]{1,0:T(8,128)} %bitcast.12), custom_call_target="tpu_custom_call" | custom-call | tf_op jit(solution)/shard_map/statistics/pallas_call | solution.py:427
  61.2 0.0 collective-permute-start
  61.2 0.0 copy-done.2
  61.2 0.6 dynamic_slice.3.listed_ref
  61.8 2.3 %collective-permute-done.incoming_ref = bf16[2,512,512]{2,1,0:T(8,128)(2,1)S(1)} collective-permute-done((bf16[2,512,512]{2,1,0:T(8,128)(2,1)}, bf16[2,512,512]{2,1,0:T(8,128)(2,1)S(1)}, u32[]{:S(2)}, u32[]{:S(2)}) %collective-permute-start) | collective-permute-done | bytes 1048608 | tf_op jit(solution)/shard_map/ppermute | solution.py:24
  64.1 0.0 copy-start
  64.1 1.0 copy-done
  65.0 54.3 %refresh.1 = (bf16[512,512]{1,0:T(8,128)(2,1)}, f32[512,512]{1,0:T(8,128)}) custom-call(s32[1]{0:T(128)} %dynamic_slice.3.listed_ref, bf16[512,512]{1,0:T(8,128)(2,1)} %get-tuple-element.17.left_ref, f32[512,512]{1,0:T(8,128)} %bitcast.14, bf16[2,512,512]{2,1,0:T(8,128)(2,1)} %copy-done), custom_call_target="tpu_custom_call" | custom-call | tf_op jit(solution)/shard_map/refresh/pallas_call | solution.py:435
  119.3 0.0 collective-permute-start.1
  119.3 2.1 %collective-permute-done.1.arrived_ref = bf16[512,512]{1,0:T(8,128)(2,1)S(1)} collective-permute-done((bf16[512,512]{1,0:T(8,128)(2,1)}, bf16[512,512]{1,0:T(8,128)(2,1)S(1)}, u32[]{:S(2)}, u32[]{:S(2)}) %collective-permute-start.1) | collective-permute-done | bytes 524320 | tf_op jit(solution)/shard_map/ppermute | solution.py:24
  121.5 0.0 copy-start.1
  121.5 0.8 copy-done.1
  122.2 8.0 %update.1 = (f32[512,512]{1,0:T(8,128)}, f32[512,512]{1,0:T(8,128)}, f32[512,512]{1,0:T(8,128)}, bf16[512,512]{1,0:T(8,128)(2,1)}) custom-call(s32[1]{0:T(128)} %dynamic_slice.3.listed_ref, bf16[512,512]{1,0:T(8,128)(2,1)} %replica_sum.1.grad_ref, f32[512,512]{1,0:T(8,128)} %bitcast.18, f32[512,512]{1,0:T(8,128)} %bitcast.19, f32[512,512]{1,0:T(8,128)} %bitcast.15, ...), custom_call_target="tpu_custom_call" | custom-call | tf_op jit(solution)/shard_map/update/pallas_call | solution.py:447
  130.3 51.2 %replica_gather.1 = bf16[8,512,512]{2,1,0:T(8,128)(2,1)} custom-call(bf16[512,512]{1,0:T(8,128)(2,1)} %get-tuple-element.21.block_ref), custom_call_target="tpu_custom_call" | custom-call | tf_op jit(solution)/shard_map/replica_gather/pallas_call | solution.py:399
  181.5 4.5 %copy.16 = bf16[8,512,512]{2,1,0:T(8,128)(2,1)} copy(bf16[8,512,512]{2,1,0:T(8,128)(2,1)} %replica_gather.1) | data formatting | bytes 8388608
Async XLA Ops:
  0.6 60.6 %copy-start.2 = (s32[32]{0:T(128)S(1)}, s32[32]{0:T(128)}, u32[]{:S(2)}) copy-start(s32[32]{0:T(128)} %param.15) | copy-start | bytes 388
  61.2 2.9 %collective-permute-start = (bf16[2,512,512]{2,1,0:T(8,128)(2,1)}, bf16[2,512,512]{2,1,0:T(8,128)(2,1)S(1)}, u32[]{:S(2)}, u32[]{:S(2)}) collective-permute-start(bf16[2,512,512]{2,1,0:T(8,128)(2,1)} %get-tuple-element.18), channel_id=1, source_target_pairs={{0,8},{8,0},{16,24},{24,16},{1,9},{9,1},{17,25},{25,17},{2,10},{10... | collective-permute-start | bytes 3145736 | tf_op jit(solution)/shard_map/ppermute | solution.py:24
  64.1 1.0 copy-start
  119.3 2.1 %collective-permute-start.1 = (bf16[512,512]{1,0:T(8,128)(2,1)}, bf16[512,512]{1,0:T(8,128)(2,1)S(1)}, u32[]{:S(2)}, u32[]{:S(2)}) collective-permute-start(bf16[512,512]{1,0:T(8,128)(2,1)} %get-tuple-element.20), channel_id=1, source_target_pairs={{0,8},{8,0},{16,24},{24,16},{1,9},{9,1},{17,25},{25,17},{2,10},{10... | collective-permute-start | bytes 1572872 | tf_op jit(solution)/shard_map/ppermute | solution.py:24
  121.5 0.8 copy-start.1
